TPU v7x, 128 devices: a whole 4x4x4 slice. The times are simulated.
128 devices in a mesh: dp: 16 (over y, x), expert: 8 (over z, core).
Axes of the slice: x: 4, y: 4, z: 4, core: 2. Of those that a mesh axis runs over, the one named last changes fastest.
Arguments:
- tokens: bfloat16 [4096, 4096], P('dp', 'expert'), may hold values from -100 to 100
- w_gate: bfloat16 [8, 4096, 14336], P('expert', None, 'dp'), may hold values from -0.09375 to 0.09375
- w_up: bfloat16 [8, 4096, 14336], P('expert', None, 'dp'), may hold values from -0.09375 to 0.09375
- w_down: bfloat16 [8, 14336, 4096], P('expert', 'dp'), may hold values from -0.046875 to 0.046875
- pick_block: int32 [8, 8], replicated, may hold values from 0 to 3
- pick_live: int32 [8, 8], replicated, may hold values from 0 to 1, as said below
- combine_weight: float32 [8, 8], replicated, may hold values from 0.25 to 1
Outputs:
- combined: bfloat16 [4096, 4096], P('dp', 'expert')
Inputs may be any that keep to these rules, and one draw needn't show every extreme that they name: `pick_live`: each expert takes at least one block, and some expert takes a block from every pair of dp rows.
All inputs are finite; a program needn't handle non-finite values.
Results may differ from a plain program's by a relative error of at most 0.02.
Values may be sent and summed in bfloat16 or wider, within the bound.
A program may use at most 128 MiB of HBM per device.

v0:
```python
import jax
import jax.numpy as jnp
from jax import lax
from jax.sharding import PartitionSpec as P

BLOCK = 128


def from_partner(value, axis, stride):
    return lax.ppermute(value, axis, [(i, i ^ 1 << stride) for i in range(lax.axis_size(axis))])


def rms_normalize(values, square_sums, model_width):
    values_f32 = values.astype(jnp.float32)
    inv_rms = lax.rsqrt(square_sums / model_width + 1e-05)
    return (values_f32 * inv_rms[:, None]).astype(jnp.bfloat16)


def on_device(tokens, w_gate, w_up, w_down, pick_block, pick_live, combine_weight):
    expert_count = lax.axis_size("expert")
    features_dev = tokens.shape[1]
    model_width = features_dev * expert_count
    blocks_here = tokens.shape[0] // BLOCK
    half_rows = BLOCK // 2
    row_index = lax.axis_index("dp")
    half_bit = row_index % 2
    pair_index = row_index // 2
    tokens_f32 = tokens.astype(jnp.float32)
    square_sums = lax.psum(jnp.sum(tokens_f32 * tokens_f32, axis=1), "expert")
    source = rms_normalize(tokens, square_sums, model_width)
    picked = lax.dynamic_index_in_dim(pick_block, pair_index, axis=1, keepdims=False)
    live_flags = lax.dynamic_index_in_dim(pick_live, pair_index, axis=1, keepdims=False)
    weights_here = lax.dynamic_index_in_dim(combine_weight, pair_index, axis=1, keepdims=False)
    owned_here = (live_flags == 1) & (picked // blocks_here == half_bit)
    local_block = picked % blocks_here
    blocks = source.reshape(blocks_here, BLOCK, features_dev)
    chosen = jnp.take(blocks, local_block, axis=0)
    chosen = jnp.where(owned_here[:, None, None], chosen, jnp.zeros((), jnp.bfloat16))
    arrived = lax.all_to_all(chosen, "expert", split_axis=0, concat_axis=2, tiled=True)[0]
    outgoing = lax.dynamic_slice_in_dim(arrived, (1 - half_bit) * half_rows, half_rows, 0)
    partner = from_partner(outgoing, "dp", 0)
    own_half = lax.dynamic_slice_in_dim(arrived, half_bit * half_rows, half_rows, 0)
    merged = own_half + partner
    gate_weights = w_gate[0]
    up_weights = w_up[0]
    down_weights = w_down[0]
    rows_piece = lax.all_gather(merged, "dp", axis=0, tiled=True)
    gate_proj = jnp.dot(rows_piece, gate_weights, preferred_element_type=jnp.float32)
    up_proj = jnp.dot(rows_piece, up_weights, preferred_element_type=jnp.float32)
    hidden = (jax.nn.silu(gate_proj) * up_proj).astype(jnp.bfloat16)
    partial_value = jnp.dot(hidden, down_weights, preferred_element_type=jnp.float32).astype(
        jnp.bfloat16
    )
    summed = lax.psum_scatter(
        lax.optimization_barrier(partial_value).astype(jnp.float32).astype(jnp.bfloat16),
        "dp",
        scatter_dimension=0,
        tiled=True,
    )
    spread = lax.all_to_all(summed[:, None, :], "expert", split_axis=2, concat_axis=1, tiled=True)
    other_half = from_partner(spread, "dp", 0)
    assembled = jnp.where(
        half_bit == 0,
        jnp.concatenate([spread, other_half], axis=0),
        jnp.concatenate([other_half, spread], axis=0),
    )
    slot_match = local_block[None, :] == jnp.arange(blocks_here, dtype=jnp.int32)[:, None]
    combine_coef = jnp.where(
        slot_match & owned_here[None, :], weights_here[None, :], jnp.zeros((), jnp.float32)
    )
    combined = jnp.einsum("le,red->lrd", combine_coef, assembled.astype(jnp.float32))
    return combined.astype(jnp.bfloat16).reshape(blocks_here * BLOCK, features_dev)


def solution(mesh):
    in_specs = (
        P("dp", "expert"),
        P("expert", None, "dp"),
        P("expert", None, "dp"),
        P("expert", "dp", None),
        P(),
        P(),
        P(),
    )
    out_specs = P("dp", "expert")
    return jax.shard_map(
        on_device, mesh=mesh, in_specs=in_specs, out_specs=out_specs, check_vma=False
    )
```

profile of v0, /device:TPU:0, one launch (start us, length us, event | category | flops | bytes accessed | tf_op | source)
XLA Modules:
  0.0 329.2 jit_solution(12364163355996505817)
XLA Ops:
  6.5 0.9 dynamic-slice_reduce_fusion.1
  7.5 1.1 fusion.12
  8.6 16.0 %psum.7 = f32[256]{0:T(256)S(1)} all-reduce(f32[256]{0:T(256)S(1)} %fusion.12), channel_id=1, replica_groups=mesh['dp'=16,'expert'=8] {'expert'}, use_global_device_ids=true, to_apply=%region_1.2 | all-reduce | flops 256 | bytes 2048 | tf_op jit(solution)/shard_map/psum | solution.py:29
  24.5 1.1 fusion.13
  25.6 0.9 fusion.15
  26.5 0.6 gather_fusion
  27.2 1.2 select_select_fusion
  28.4 3.6 %all-to-all-start = ((bf16[8,128,512]{2,1,0:T(8,128)(2,1)}), bf16[8,128,512]{2,1,0:T(8,128)(2,1)S(1)}, u32[]{:S(2)}, u32[]{:S(2)}) async-start(bf16[8,128,512]{2,1,0:T(8,128)(2,1)} %select_select_fusion), calls=%async_computation | async-start | bytes 2097152 | tf_op jit(solution)/shard_map/all_to_all | solution.py:39
  32.0 15.8 %all-to-all-done = bf16[8,128,512]{2,1,0:T(8,128)(2,1)S(1)} async-done(((bf16[8,128,512]{2,1,0:T(8,128)(2,1)}), bf16[8,128,512]{2,1,0:T(8,128)(2,1)S(1)}, u32[]{:S(2)}, u32[]{:S(2)}) %all-to-all-start) | async-done | bytes 1048608 | tf_op jit(solution)/shard_map/all_to_all | solution.py:39
  47.8 0.7 copy.27
  48.5 0.6 constant_dynamic-slice_fusion
  49.1 0.4 copy.29
  49.5 1.6 collective-permute-start
  51.0 0.4 copy.33
  51.4 11.6 %collective-permute-done = bf16[64,4096]{1,0:T(8,128)(2,1)S(1)} collective-permute-done((bf16[64,4096]{1,0:T(8,128)(2,1)S(1)}, bf16[64,4096]{1,0:T(8,128)(2,1)S(1)}, u32[]{:S(2)}, u32[]{:S(2)}) %collective-permute-start) | collective-permute-done | bytes 524320 | tf_op jit(solution)/shard_map/ppermute | solution.py:10
  63.0 1.0 add.73
  64.2 70.0 %all-gather.2.cloned.1.call-done = bf16[1024,4096]{1,0:T(8,128)(2,1)} async-done(((bf16[64,4096]{1,0:T(8,128)(2,1)}), bf16[1024,4096]{1,0:T(8,128)(2,1)}) %all-gather.2.cloned.1.call-update) | async-done | bytes 8388624 | tf_op jit(solution)/shard_map/all_gather | solution.py:47
  134.3 12.5 %fusion.1 = f32[1024,896]{1,0:T(8,128)S(1)} fusion(bf16[1024,4096]{1,0:T(8,128)(2,1)} %all-gather.2.cloned.1.call-done, bf16[1,4096,896]{2,1,0:T(8,128)(2,1)} %param.9), kind=kOutput, calls=%fused_computation.3 | convolution fusion | flops 7516192768 | bytes 19398656 | tf_op jit(solution)/shard_map/dot_general | solution.py:49
  146.8 15.1 %fusion.3 = f32[1024,896]{1,0:T(8,128)S(1)} fusion(bf16[1024,4096]{1,0:T(8,128)(2,1)S(1)} %copy-done.1, bf16[1,4096,896]{2,1,0:T(8,128)(2,1)} %param.8), kind=kOutput, calls=%fused_computation.5 | convolution fusion | flops 7516192768 | bytes 19398656 | tf_op jit(solution)/shard_map/dot_general | solution.py:48
  161.9 14.1 %convolution_convert_fusion = bf16[1024,4096]{1,0:T(8,128)(2,1)} fusion(bf16[1,896,4096]{2,1,0:T(8,128)(2,1)} %param.10, f32[1024,896]{1,0:T(8,128)S(1)} %fusion.1, f32[1024,896]{1,0:T(8,128)S(1)} %fusion.3), kind=kOutput, calls=%fused_computation.1 | convolution fusion | flops 7525892096 | bytes 23068672 | tf_op jit(solution)/shard_map/dot_general | solution.py:51
  176.0 84.8 %reduce-scatter.2.cloned.1.call-done = bf16[64,4096]{1,0:T(8,128)(2,1)} async-done(((bf16[1024,4096]{1,0:T(8,128)(2,1)}), bf16[64,4096]{1,0:T(8,128)(2,1)}) %reduce-scatter.2.cloned.1.call-update) | async-done | bytes 524304 | tf_op jit(solution)/shard_map/reduce_scatter | solution.py:54
  260.7 4.9 %copy.30 = bf16[64,1,4096]{0,1,2:T(2,128)(2,1)S(1)} copy(bf16[64,1,4096]{2,0,1:T(8,128)(2,1)} %bitcast.33) | data formatting | bytes 1048576 | tf_op jit(solution)/shard_map/broadcast_in_dim | solution.py:60
  265.6 0.5 broadcast.170
  266.1 22.6 %reduce.10 = bf16[4096,64]{1,0:T(8,128)(2,1)S(1)} reduce(bf16[4096,1,64]{2,1,0:T(2,128)(2,1)S(1)} %bitcast.29, bf16[]{:T(256)} %broadcast.170), dimensions={1}, to_apply=%bitcast.23.reduce_sub_computation | reduce | bytes 1048578
  288.8 0.7 reshape.126
  289.5 14.6 %all_to_all.27 = bf16[8,2,16384]{2,1,0:T(2,128)(2,1)S(1)} all-to-all(bf16[8,2,16384]{2,1,0:T(2,128)(2,1)S(1)} %reshape.126), channel_id=1, replica_groups=mesh['dp'=16,'expert'=8] {'expert'}, dimensions={0} | all-to-all | bytes 1048576 | tf_op jit(solution)/shard_map/all_to_all | solution.py:60
  304.1 1.2 reshape.127
  305.4 2.3 copy.31
  307.8 1.5 collective-permute-start.1
  309.5 11.7 %collective-permute-done.1 = bf16[64,8,512]{2,1,0:T(8,128)(2,1)S(1)} collective-permute-done((bf16[64,8,512]{2,1,0:T(8,128)(2,1)S(1)}, bf16[64,8,512]{2,1,0:T(8,128)(2,1)S(1)}, u32[]{:S(2)}, u32[]{:S(2)}) %collective-permute-start.1) | collective-permute-done | bytes 524320 | tf_op jit(solution)/shard_map/ppermute | solution.py:10
  321.2 0.4 convolution_convert_fusion.1
  321.6 0.7 copy.32
  (14 shorter events, 0.7 us)
Async XLA Ops:
  6.5 302.8 %copy-start = (f32[8,8]{1,0:T(8,128)S(1)}, f32[8,8]{1,0:T(8,128)}, u32[]{:S(2)}) copy-start(f32[8,8]{1,0:T(8,128)} %param.13) | copy-start | bytes 772
  28.4 19.4 %all-to-all-start = ((bf16[8,128,512]{2,1,0:T(8,128)(2,1)}), bf16[8,128,512]{2,1,0:T(8,128)(2,1)S(1)}, u32[]{:S(2)}, u32[]{:S(2)}) async-start(bf16[8,128,512]{2,1,0:T(8,128)(2,1)} %select_select_fusion), calls=%async_computation | async-start | bytes 2097152 | tf_op jit(solution)/shard_map/all_to_all | solution.py:39
  31.9 102.4 %all-gather.2.cloned.1.call-start = ((), (), s32[]{:S(2)}) async-start(), calls=%async_computation.3 | async-start | bytes 8912896 | tf_op jit(solution)/shard_map/all_gather | solution.py:47
  49.5 13.5 %collective-permute-start = (bf16[64,4096]{1,0:T(8,128)(2,1)S(1)}, bf16[64,4096]{1,0:T(8,128)(2,1)S(1)}, u32[]{:S(2)}, u32[]{:S(2)}) collective-permute-start(bf16[64,4096]{1,0:T(8,128)(2,1)S(1)} %copy.29), channel_id=1, source_target_pairs={{0,8},{8,0},{16,24},{24,16},{32,40},{40,32},{48,56},{56,48},{64,72... | collective-permute-start | bytes 1572872 | tf_op jit(solution)/shard_map/ppermute | solution.py:10
  64.0 196.7 %reduce-scatter.2.cloned.1.call-start = ((), (), s32[]{:S(2)}) async-start(), calls=%async_computation.4 | async-start | bytes 8912896 | tf_op jit(solution)/shard_map/reduce_scatter | solution.py:54
  134.3 12.5 %copy-start.1 = (bf16[1024,4096]{1,0:T(8,128)(2,1)S(1)}, bf16[1024,4096]{1,0:T(8,128)(2,1)}, u32[]{:S(2)}) copy-start(bf16[1024,4096]{1,0:T(8,128)(2,1)} %all-gather.2.cloned.1.call-done) | copy-start | bytes 25165828
  307.8 13.4 %collective-permute-start.1 = (bf16[64,8,512]{2,1,0:T(8,128)(2,1)S(1)}, bf16[64,8,512]{2,1,0:T(8,128)(2,1)S(1)}, u32[]{:S(2)}, u32[]{:S(2)}) collective-permute-start(bf16[64,8,512]{2,1,0:T(8,128)(2,1)S(1)} %bitcast.34), channel_id=1, source_target_pairs={{0,8},{8,0},{16,24},{24,16},{32,40},{40,32},{48,56},{56,48},{64,72... | collective-permute-start | bytes 1572872 | tf_op jit(solution)/shard_map/ppermute | solution.py:10
Sparse Core Ops, SparseCore 0:
  64.1 70.0 all-gather.1
  176.1 84.5 reduce-scatter.1
where the time goes:
time: 330 us; the launch traced here: 329 us
  waiting for transfers between devices  194 us (59%)
  matrix products  42.1 us (13%)
  blocking collectives  30.6 us (9%)
  other arithmetic  28.8 us (9%)
  between operations  13.6 us (4%)
  local copies, waits for them, and re-layouts  13.3 us (4%)
  starting transfers between devices  6.86 us (2%)
    reduce_scatter x1, waiting for transfers between devices, on_device(): lax.psum_scatter(lax.optimization_barrier(partial_value).astype(jnp.float...  84.8 us
    all_gather x1, waiting for transfers between devices, on_device(): rows_piece = lax.all_gather(merged, 'dp', axis=0, tiled=True)  70 us
    ppermute x2, waiting for transfers between devices, from_partner(): lax.ppermute(value, axis, [(i, i ^ 1 << stride) for i in range(lax.axis_s...  23.3 us
    unnamed x1, other arithmetic  22.6 us
    psum x1, blocking collectives, on_device(): square_sums = lax.psum(jnp.sum(tokens_f32 * tokens_f32, axis=1), 'expert')  16 us
    all_to_all x1, waiting for transfers between devices, on_device(): lax.all_to_all(chosen, 'expert', split_axis=0, concat_axis=2, tiled=True)[0]  15.8 us
    dot_general x1, matrix products, on_device(): jnp.dot(rows_piece, gate_weights, preferred_element_type=jnp.float32)  15.1 us
    all_to_all x1, blocking collectives, on_device(): lax.all_to_all(summed[:, None, :], 'expert', split_axis=2, concat_axis=1,...  14.6 us
  transfers between devices with their start and end apart: 5, of which 5 were waited for; matrix products, arithmetic and copies ran while one was open for 0% of the time, Pallas kernels for 0%

commit v1 on v0

v1 whole, which is shorter than its diff:
```python
import functools

import jax
import jax.numpy as jnp
from jax import lax
from jax.experimental import pallas as pl
from jax.experimental.pallas import tpu as pltpu
from jax.sharding import PartitionSpec as P

BLOCK = 128
HALF = BLOCK // 2
SUB = 16
RING = 4
BF16 = jnp.bfloat16
F32 = jnp.float32


def layer_kernel(
    expert_count,
    tok,
    w_gate,
    w_up,
    w_down,
    pick,
    live,
    weight,
    out,
    pair_buf,
    send_buf,
    arrived,
    rows,
    w_gu,
    w_dn,
    hidden,
    part,
    from_minus,
    from_plus,
    far_minus,
    far_plus,
    mid,
    mid_minus,
    mid_plus,
    mid_far_minus,
    mid_far_plus,
    finished,
    returned,
    merged,
    send_sem,
    recv_sem,
    weight_sem,
    local_sem,
):
    position = lax.axis_index("dp")
    expert = lax.axis_index("expert")
    x = lax.rem(position, RING)
    y = position // RING
    half = lax.rem(position, 2)
    pair = position // 2
    partner = position + 1 - 2 * half
    x_plus = y * RING + lax.rem(x + 1, RING)
    x_minus = y * RING + lax.rem(x + RING - 1, RING)
    y_plus = lax.rem(y + 1, RING) * RING + x
    y_minus = lax.rem(y + RING - 1, RING) * RING + x
    near = ((x_plus, x_minus), (y_plus, y_minus))
    wide = ((y_plus, y_minus), (x_plus, x_minus))
    lanes = tok.shape[-1]
    width = lanes * expert_count
    hid_tiles = w_gate.shape[1] // 128
    peers = (4, 3, 5, 2, 6, 1, 7)

    weight_copies = []
    for tile in range(hid_tiles):
        for which, source in enumerate((w_gate, w_up)):
            weight_copies.append(
                pltpu.make_async_copy(
                    source.at[:, pl.ds(tile * 128, 128)],
                    w_gu.at[tile, :, pl.ds(which * 128, 128)],
                    weight_sem.at[2 * tile + which],
                )
            )
    weight_copies.append(pltpu.make_async_copy(w_down, w_dn, weight_sem.at[2 * hid_tiles]))

    barrier = pltpu.get_barrier_semaphore()
    for target in (x_plus, x_minus, y_plus, y_minus):
        pl.semaphore_signal(
            barrier, inc=1, device_id={"dp": target}, device_id_type=pl.DeviceIdType.MESH
        )
    for offset in peers:
        pl.semaphore_signal(
            barrier,
            inc=1,
            device_id={"expert": lax.rem(expert + offset, expert_count)},
            device_id_type=pl.DeviceIdType.MESH,
        )
    pl.semaphore_wait(barrier, 4 + len(peers))

    copies = {}

    def send(key, source, target, device):
        number = len(copies)
        copy = pltpu.make_async_remote_copy(
            src_ref=source,
            dst_ref=target,
            send_sem=send_sem.at[number],
            recv_sem=recv_sem.at[number],
            device_id=device,
            device_id_type=pl.DeviceIdType.MESH,
        )
        copy.start()
        copies[key] = copy

    def arrive(*key):
        copies[key].wait_recv()

    send(("pair",), tok.at[:, 1 - half], pair_buf.at[pl.ds(2 * half, 2)], {"dp": partner})
    own_copy = pltpu.make_async_copy(
        tok.at[:, half], pair_buf.at[pl.ds(2 * half, 2)], local_sem.at[0]
    )
    own_copy.start()
    for copy in weight_copies:
        copy.start()
    own_copy.wait()
    arrive("pair")

    def choose(target):
        chosen = pair_buf[pick[target, pair]].astype(F32)
        return (chosen * live[target, pair].astype(F32)).astype(BF16)

    for offset in peers:
        target = lax.rem(expert + offset, expert_count)
        send_buf[offset] = choose(target)
        send(("out", offset), send_buf.at[offset], arrived.at[expert], {"expert": target})
    arrived[expert] = choose(expert)
    for offset in peers:
        arrive("out", offset)

    for piece in range(HALF // SUB):
        square_sum = jnp.zeros((SUB, 1), F32)
        for source in range(expert_count):
            values = arrived[source, pl.ds(piece * SUB, SUB)].astype(F32)
            square_sum += jnp.sum(values * values, axis=1, keepdims=True)
        inv_rms = lax.rsqrt(square_sum / width + 1e-05)
        for source in range(expert_count):
            values = arrived[source, pl.ds(piece * SUB, SUB)].astype(F32)
            rows[0, piece // 2, 0, piece % 2, :, pl.ds(source * lanes, lanes)] = (
                values * inv_rms
            ).astype(BF16)

    def spread_wide(c, r):
        send(("rows", 2, c, r), rows.at[0, c, r], rows.at[2, c, r], {"dp": wide[c][0]})
        send(("rows", 1, c, r), rows.at[0, c, r], rows.at[1, c, r], {"dp": wide[c][1]})

    def forward_wide(c, r):
        arrive("rows", 2, c, r)
        send(("far", c, r, 0), rows.at[2, c, r, 0], rows.at[3, c, r, 0], {"dp": wide[c][0]})
        arrive("rows", 1, c, r)
        send(("far", c, r, 1), rows.at[1, c, r, 1], rows.at[3, c, r, 1], {"dp": wide[c][1]})

    def experts(s):
        def gate_up(tile, carry):
            group = rows[s].reshape(2 * RING * 2 * SUB, width)
            both = jnp.dot(group, w_gu[tile], preferred_element_type=F32)
            gate = both[:, :128]
            value = gate * (1.0 / (1.0 + jnp.exp(-gate))) * both[:, 128:]
            hidden[:, pl.ds(pl.multiple_of(tile * 128, 128), 128)] = value.astype(BF16)
            return carry

        lax.fori_loop(0, hid_tiles, gate_up, 0)

        def down(tile, carry):
            columns = pl.ds(pl.multiple_of(tile * 512, 512), 512)
            value = jnp.dot(hidden[...], w_dn[:, columns], preferred_element_type=F32)
            part[s, :, :, :, :, columns] = value.astype(BF16).reshape(2, RING, 2, SUB, 512)
            return carry

        lax.fori_loop(0, width // 512, down, 0)

    for c in range(2):
        send(("near", c, 2), rows.at[0, c, 0], rows.at[0, c, 2], {"dp": near[c][0]})
        send(("near", c, 1), rows.at[0, c, 0], rows.at[0, c, 1], {"dp": near[c][1]})
    for c in range(2):
        spread_wide(c, 0)
    for c in range(2):
        arrive("near", c, 2)
        send(("nearfar", c, 0), rows.at[0, c, 2, 0], rows.at[0, c, 3, 0], {"dp": near[c][0]})
        arrive("near", c, 1)
        send(("nearfar", c, 1), rows.at[0, c, 1, 1], rows.at[0, c, 3, 1], {"dp": near[c][1]})
    for r in (1, 2):
        for c in range(2):
            spread_wide(c, r)
    for c in range(2):
        arrive("nearfar", c, 0)
        arrive("nearfar", c, 1)
        spread_wide(c, 3)
    for c in range(2):
        forward_wide(c, 0)
    for copy in weight_copies:
        copy.wait()
    experts(0)
    for r in (1, 2, 3):
        for c in range(2):
            forward_wide(c, r)
    experts(1)
    for c in range(2):
        send(("half", c, 1), part.at[1, c, :, 1], from_minus.at[c, :, 1], {"dp": wide[c][0]})
    experts(2)
    for c in range(2):
        send(("half", c, 0), part.at[2, c, :, 0], from_plus.at[c, :, 0], {"dp": wide[c][1]})
    for r in range(RING):
        for c in range(2):
            arrive("far", c, r, 0)
            arrive("far", c, r, 1)
    experts(3)
    order = (3, 1, 2, 0)
    for r in order:
        for c in range(2):
            send(("sumfar", c, r, 0), part.at[3, c, r, 0], far_minus.at[c, r], {"dp": wide[c][0]})
            send(("sumfar", c, r, 1), part.at[3, c, r, 1], far_plus.at[c, r], {"dp": wide[c][1]})
    for r in order:
        for c in range(2):
            arrive("sumfar", c, r, 0)
            part[1, c, r, 0] = (part[1, c, r, 0].astype(F32) + far_minus[c, r].astype(F32)).astype(
                BF16
            )
            send(
                ("sum", c, r, 0), part.at[1, c, r, 0], from_minus.at[c, r, 0], {"dp": wide[c][0]}
            )
            arrive("sumfar", c, r, 1)
            part[2, c, r, 1] = (part[2, c, r, 1].astype(F32) + far_plus[c, r].astype(F32)).astype(
                BF16
            )
            send(("sum", c, r, 1), part.at[2, c, r, 1], from_plus.at[c, r, 1], {"dp": wide[c][1]})
    for c in range(2):
        arrive("half", c, 1)
        arrive("half", c, 0)

    def row_sum(c, r, piece):
        return (
            part[0, c, r, piece].astype(F32)
            + from_minus[c, r, piece].astype(F32)
            + from_plus[c, r, piece].astype(F32)
        )

    for c in range(2):
        arrive("sum", c, 3, 0)
        arrive("sum", c, 3, 1)
        for piece in range(2):
            mid[c, 3, piece] = row_sum(c, 3, piece).astype(BF16)
            target = (mid_far_minus, mid_far_plus)[piece]
            send(("midfar", c, piece), mid.at[c, 3, piece], target.at[c], {"dp": near[c][piece]})
    for c in range(2):
        arrive("sum", c, 1, 0)
        arrive("sum", c, 1, 1)
        mid[c, 1, 1] = row_sum(c, 1, 1).astype(BF16)
        send(("mid", c, 1), mid.at[c, 1, 1], mid_minus.at[c, 1], {"dp": near[c][0]})
        arrive("sum", c, 2, 0)
        arrive("sum", c, 2, 1)
        mid[c, 2, 0] = row_sum(c, 2, 0).astype(BF16)
        send(("mid", c, 0), mid.at[c, 2, 0], mid_plus.at[c, 0], {"dp": near[c][1]})
    for c in range(2):
        arrive("midfar", c, 0)
        mid[c, 1, 0] = (row_sum(c, 1, 0) + mid_far_minus[c].astype(F32)).astype(BF16)
        send(("midsum", c, 0), mid.at[c, 1, 0], mid_minus.at[c, 0], {"dp": near[c][0]})
        arrive("midfar", c, 1)
        mid[c, 2, 1] = (row_sum(c, 2, 1) + mid_far_plus[c].astype(F32)).astype(BF16)
        send(("midsum", c, 1), mid.at[c, 2, 1], mid_plus.at[c, 1], {"dp": near[c][1]})
    for c in range(2):
        arrive("sum", c, 0, 0)
        arrive("sum", c, 0, 1)
        arrive("mid", c, 0)
        arrive("mid", c, 1)
        arrive("midsum", c, 0)
        arrive("midsum", c, 1)
        for piece in range(2):
            total = (
                row_sum(c, 0, piece)
                + mid_minus[c, piece].astype(F32)
                + mid_plus[c, piece].astype(F32)
            ).astype(BF16)
            first_row = (2 * c + piece) * SUB
            for target in range(expert_count):
                finished[target, pl.ds(first_row, SUB)] = total[
                    :, target * lanes : (target + 1) * lanes
                ]

    for offset in peers:
        target = lax.rem(expert + offset, expert_count)
        send(("back", offset), finished.at[target], returned.at[expert], {"expert": target})
    returned[expert] = finished[expert]
    for offset in peers:
        arrive("back", offset)

    for piece in range(HALF // SUB):
        window = pl.ds(piece * SUB, SUB)
        totals = [jnp.zeros((SUB, lanes), F32) for _ in range(4)]
        for source in range(expert_count):
            values = returned[source, window].astype(F32)
            block = pick[source, pair]
            scale = jnp.where(live[source, pair] == 1, weight[source, pair], 0.0)
            for slot in range(4):
                totals[slot] = totals[slot] + jnp.where(block == slot, scale, 0.0) * values
        for slot in range(4):
            merged[slot, window] = totals[slot].astype(BF16)
    send(
        ("final",), merged.at[pl.ds(2 * (1 - half), 2)], out.at[:, half], {"dp": partner}
    )
    last_copy = pltpu.make_async_copy(
        merged.at[pl.ds(2 * half, 2)], out.at[:, half], local_sem.at[1]
    )
    last_copy.start()
    for key, copy in copies.items():
        copy.wait_send()
    last_copy.wait()
    arrive("final")


def on_device(tokens, w_gate, w_up, w_down, pick_block, pick_live, combine_weight):
    expert_count = lax.axis_size("expert")
    lanes = tokens.shape[1]
    width = lanes * expert_count
    group = w_gate.shape[2]
    hid_tiles = group // 128
    hbm = pl.BlockSpec(memory_space=pl.ANY)
    smem = pl.BlockSpec(memory_space=pltpu.SMEM)
    copy_count = 128
    result = pl.pallas_call(
        functools.partial(layer_kernel, expert_count),
        out_shape=jax.ShapeDtypeStruct((2, 2, HALF, lanes), BF16),
        in_specs=[hbm, hbm, hbm, hbm, smem, smem, smem],
        out_specs=hbm,
        scratch_shapes=[
            pltpu.VMEM((4, HALF, lanes), BF16),
            pltpu.VMEM((expert_count, HALF, lanes), BF16),
            pltpu.VMEM((expert_count, HALF, lanes), BF16),
            pltpu.VMEM((RING, 2, RING, 2, SUB, width), BF16),
            pltpu.VMEM((hid_tiles, width, 256), BF16),
            pltpu.VMEM((group, width), BF16),
            pltpu.VMEM((2 * RING * 2 * SUB, group), BF16),
            pltpu.VMEM((RING, 2, RING, 2, SUB, width), BF16),
            pltpu.VMEM((2, RING, 2, SUB, width), BF16),
            pltpu.VMEM((2, RING, 2, SUB, width), BF16),
            pltpu.VMEM((2, RING, SUB, width), BF16),
            pltpu.VMEM((2, RING, SUB, width), BF16),
            pltpu.VMEM((2, RING, 2, SUB, width), BF16),
            pltpu.VMEM((2, 2, SUB, width), BF16),
            pltpu.VMEM((2, 2, SUB, width), BF16),
            pltpu.VMEM((2, SUB, width), BF16),
            pltpu.VMEM((2, SUB, width), BF16),
            pltpu.VMEM((expert_count, HALF, lanes), BF16),
            pltpu.VMEM((expert_count, HALF, lanes), BF16),
            pltpu.VMEM((4, HALF, lanes), BF16),
            pltpu.SemaphoreType.DMA((copy_count,)),
            pltpu.SemaphoreType.DMA((copy_count,)),
            pltpu.SemaphoreType.DMA((2 * hid_tiles + 1,)),
            pltpu.SemaphoreType.DMA((2,)),
        ],
        compiler_params=pltpu.CompilerParams(
            collective_id=0, has_side_effects=True, vmem_limit_bytes=60 * 1024 * 1024
        ),
        name="moe_layer",
    )(
        tokens.reshape(2, 2, HALF, lanes),
        w_gate[0],
        w_up[0],
        w_down[0],
        pick_block,
        pick_live,
        combine_weight,
    )
    return result.reshape(tokens.shape)


def solution(mesh):
    in_specs = (
        P("dp", "expert"),
        P("expert", None, "dp"),
        P("expert", None, "dp"),
        P("expert", "dp", None),
        P(),
        P(),
        P(),
    )
    return jax.shard_map(
        on_device, mesh=mesh, in_specs=in_specs, out_specs=P("dp", "expert"), check_vma=False
    )
```

time: 330 us -> 132 us (0.40)
  waiting for transfers between devices: 194 us -> 0 us
  Pallas kernels: 0 us -> 130 us
  matrix products: 42.1 us -> 0 us
  blocking collectives: 30.6 us -> 0 us
  other arithmetic: 28.8 us -> 0 us
  between operations: 13.6 us -> 0.01 us
  local copies, waits for them, and re-layouts: 13.3 us -> 1.67 us
  starting transfers between devices: 6.86 us -> 0 us
    pallas_call x0 -> x1, Pallas kernels: none -> 130 us  [on_device(): pl.pallas_call(functools.partial(layer_kernel, expert_count), out_shape=j...]
    reduce_scatter x1 -> x0, waiting for transfers between devices: 84.8 us -> none  [on_device(): lax.psum_scatter(lax.optimization_barrier(partial_value).astype(jnp.float...]
    all_gather x1 -> x0, waiting for transfers between devices: 70 us -> none  [on_device(): rows_piece = lax.all_gather(merged, 'dp', axis=0, tiled=True)]
    dot_general x4 -> x0, matrix products: 42.1 us -> none  [the longest x1 15.1 us: on_device(): jnp.dot(rows_piece, gate_weights, preferred_element_type=jnp.float32)]
    ppermute x2 -> x0, waiting for transfers between devices: 23.3 us -> none  [from_partner(): lax.ppermute(value, axis, [(i, i ^ 1 << stride) for i in range(lax.axis_s...]
    unnamed x1 -> x0, other arithmetic: 22.6 us -> none
    psum x1 -> x0, blocking collectives: 16 us -> none  [on_device(): square_sums = lax.psum(jnp.sum(tokens_f32 * tokens_f32, axis=1), 'expert')]
    all_to_all x1 -> x0, waiting for transfers between devices: 15.8 us -> none  [on_device(): lax.all_to_all(chosen, 'expert', split_axis=0, concat_axis=2, tiled=True)[0]]
  transfers between devices with their start and end apart: 5 -> 0, of which waited for: 5 -> 0; matrix products, arithmetic and copies ran while one was open for 0% -> 0% of each run, Pallas kernels for 0% -> 0%
where the time goes in v1:
time: 132 us; the launch traced here: 131 us
  Pallas kernels  130 us (98%)
  local copies, waits for them, and re-layouts  1.67 us (1%)
    pallas_call x1, Pallas kernels, on_device(): pl.pallas_call(functools.partial(layer_kernel, expert_count), out_shape=j...  130 us

profile of v1, /device:TPU:0, one launch (start us, length us, event | category | flops | bytes accessed | tf_op | source)
XLA Modules:
  0.0 131.4 jit_solution(6702122422840011697)
XLA Ops:
  0.0 129.7 %moe_layer.1 = bf16[2,2,64,512]{3,2,1,0:T(8,128)(2,1)} custom-call(bf16[2,2,64,512]{3,2,1,0:T(8,128)(2,1)} %bitcast.9, bf16[4096,896]{1,0:T(8,128)(2,1)} %bitcast.5, bf16[4096,896]{1,0:T(8,128)(2,1)} %bitcast.6, bf16[896,4096]{1,0:T(8,128)(2,1)} %bitcast.7, s32[8,8]{1,0:T(8,128)} %pick.1, s32[8,8]{1,0:T(8,128)} %live.1, f32[8,8]{1,0:T(8,128)} %weight.1), custom_call_target="tpu_custom_call" | custom-call | tf_op jit(solution)/shard_map/moe_layer/pallas_call | solution.py:326
  129.7 1.7 %copy.9 = bf16[256,512]{1,0:T(8,128)(2,1)} copy(bf16[256,512]{1,0:T(8,128)(2,1)} %bitcast.8) | data formatting | bytes 524288

commit v2 on v1

--- a/solution.py
+++ b/solution.py
@@ -11,6 +11,7 @@
 HALF = BLOCK // 2
 SUB = 16
 RING = 4
+DOWN = 512
 BF16 = jnp.bfloat16
 F32 = jnp.float32
 
@@ -25,7 +26,8 @@
     live,
     weight,
     out,
-    pair_buf,
+    pair_first,
+    pair_second,
     send_buf,
     arrived,
     rows,
@@ -80,6 +82,7 @@
             )
     weight_copies.append(pltpu.make_async_copy(w_down, w_dn, weight_sem.at[2 * hid_tiles]))
 
+    pair_bufs = (pair_first, pair_second)
     barrier = pltpu.get_barrier_semaphore()
     for target in (x_plus, x_minus, y_plus, y_minus):
         pl.semaphore_signal(
@@ -112,39 +115,55 @@
     def arrive(*key):
         copies[key].wait_recv()
 
-    send(("pair",), tok.at[:, 1 - half], pair_buf.at[pl.ds(2 * half, 2)], {"dp": partner})
-    own_copy = pltpu.make_async_copy(
-        tok.at[:, half], pair_buf.at[pl.ds(2 * half, 2)], local_sem.at[0]
-    )
-    own_copy.start()
+    for c in range(2):
+        send(
+            ("pair", c),
+            tok.at[:, 1 - half, c],
+            pair_bufs[c].at[pl.ds(2 * half, 2)],
+            {"dp": partner},
+        )
+    own_copies = [
+        pltpu.make_async_copy(
+            tok.at[:, half, c], pair_bufs[c].at[pl.ds(2 * half, 2)], local_sem.at[c]
+        )
+        for c in range(2)
+    ]
+    for copy in own_copies:
+        copy.start()
+
+    def choose(target, c):
+        chosen = pair_bufs[c][pick[target, pair]].astype(F32)
+        return (chosen * live[target, pair].astype(F32)).astype(BF16)
+
+    for c in range(2):
+        own_copies[c].wait()
+        arrive("pair", c)
+        for offset in peers:
+            target = lax.rem(expert + offset, expert_count)
+            send_buf[c, offset] = choose(target, c)
+            send(
+                ("out", c, offset),
+                send_buf.at[c, offset],
+                arrived.at[c, expert],
+                {"expert": target},
+            )
+        arrived[c, expert] = choose(expert, c)
     for copy in weight_copies:
         copy.start()
-    own_copy.wait()
-    arrive("pair")
-
-    def choose(target):
-        chosen = pair_buf[pick[target, pair]].astype(F32)
-        return (chosen * live[target, pair].astype(F32)).astype(BF16)
-
-    for offset in peers:
-        target = lax.rem(expert + offset, expert_count)
-        send_buf[offset] = choose(target)
-        send(("out", offset), send_buf.at[offset], arrived.at[expert], {"expert": target})
-    arrived[expert] = choose(expert)
-    for offset in peers:
-        arrive("out", offset)
-
-    for piece in range(HALF // SUB):
-        square_sum = jnp.zeros((SUB, 1), F32)
-        for source in range(expert_count):
-            values = arrived[source, pl.ds(piece * SUB, SUB)].astype(F32)
-            square_sum += jnp.sum(values * values, axis=1, keepdims=True)
-        inv_rms = lax.rsqrt(square_sum / width + 1e-05)
-        for source in range(expert_count):
-            values = arrived[source, pl.ds(piece * SUB, SUB)].astype(F32)
-            rows[0, piece // 2, 0, piece % 2, :, pl.ds(source * lanes, lanes)] = (
-                values * inv_rms
-            ).astype(BF16)
+
+    def normalise(c):
+        for piece in range(2):
+            window = pl.ds(piece * SUB, SUB)
+            square_sum = jnp.zeros((SUB, 1), F32)
+            for source in range(expert_count):
+                values = arrived[c, source, window].astype(F32)
+                square_sum += jnp.sum(values * values, axis=1, keepdims=True)
+            inv_rms = lax.rsqrt(square_sum / width + 1e-05)
+            for source in range(expert_count):
+                values = arrived[c, source, window].astype(F32)
+                rows[0, c, 0, piece, :, pl.ds(source * lanes, lanes)] = (values * inv_rms).astype(
+                    BF16
+                )
 
     def spread_wide(c, r):
         send(("rows", 2, c, r), rows.at[0, c, r], rows.at[2, c, r], {"dp": wide[c][0]})
@@ -157,28 +176,23 @@
         send(("far", c, r, 1), rows.at[1, c, r, 1], rows.at[3, c, r, 1], {"dp": wide[c][1]})
 
     def experts(s):
-        def gate_up(tile, carry):
-            group = rows[s].reshape(2 * RING * 2 * SUB, width)
+        group = rows[s].reshape(2 * RING * 2 * SUB, width)
+        for tile in range(hid_tiles):
             both = jnp.dot(group, w_gu[tile], preferred_element_type=F32)
             gate = both[:, :128]
             value = gate * (1.0 / (1.0 + jnp.exp(-gate))) * both[:, 128:]
-            hidden[:, pl.ds(pl.multiple_of(tile * 128, 128), 128)] = value.astype(BF16)
-            return carry
-
-        lax.fori_loop(0, hid_tiles, gate_up, 0)
-
-        def down(tile, carry):
-            columns = pl.ds(pl.multiple_of(tile * 512, 512), 512)
+            hidden[:, tile * 128 : (tile + 1) * 128] = value.astype(BF16)
+        for tile in range(width // DOWN):
+            columns = pl.ds(tile * DOWN, DOWN)
             value = jnp.dot(hidden[...], w_dn[:, columns], preferred_element_type=F32)
-            part[s, :, :, :, :, columns] = value.astype(BF16).reshape(2, RING, 2, SUB, 512)
-            return carry
-
-        lax.fori_loop(0, width // 512, down, 0)
-
-    for c in range(2):
+            part[s, :, :, :, :, columns] = value.astype(BF16).reshape(2, RING, 2, SUB, DOWN)
+
+    for c in range(2):
+        for offset in peers:
+            arrive("out", c, offset)
+        normalise(c)
         send(("near", c, 2), rows.at[0, c, 0], rows.at[0, c, 2], {"dp": near[c][0]})
         send(("near", c, 1), rows.at[0, c, 0], rows.at[0, c, 1], {"dp": near[c][1]})
-    for c in range(2):
         spread_wide(c, 0)
     for c in range(2):
         arrive("near", c, 2)
@@ -277,41 +291,52 @@
                 + mid_minus[c, piece].astype(F32)
                 + mid_plus[c, piece].astype(F32)
             ).astype(BF16)
-            first_row = (2 * c + piece) * SUB
             for target in range(expert_count):
-                finished[target, pl.ds(first_row, SUB)] = total[
+                finished[c, target, pl.ds(piece * SUB, SUB)] = total[
                     :, target * lanes : (target + 1) * lanes
                 ]
-
-    for offset in peers:
-        target = lax.rem(expert + offset, expert_count)
-        send(("back", offset), finished.at[target], returned.at[expert], {"expert": target})
-    returned[expert] = finished[expert]
-    for offset in peers:
-        arrive("back", offset)
-
-    for piece in range(HALF // SUB):
-        window = pl.ds(piece * SUB, SUB)
-        totals = [jnp.zeros((SUB, lanes), F32) for _ in range(4)]
-        for source in range(expert_count):
-            values = returned[source, window].astype(F32)
-            block = pick[source, pair]
-            scale = jnp.where(live[source, pair] == 1, weight[source, pair], 0.0)
+        for offset in peers:
+            target = lax.rem(expert + offset, expert_count)
+            send(
+                ("back", c, offset),
+                finished.at[c, target],
+                returned.at[c, expert],
+                {"expert": target},
+            )
+        returned[c, expert] = finished[c, expert]
+
+    last_copies = []
+    for c in range(2):
+        for offset in peers:
+            arrive("back", c, offset)
+        for piece in range(2):
+            window = pl.ds(piece * SUB, SUB)
+            totals = [jnp.zeros((SUB, lanes), F32) for _ in range(4)]
+            for source in range(expert_count):
+                values = returned[c, source, window].astype(F32)
+                block = pick[source, pair]
+                scale = jnp.where(live[source, pair] == 1, weight[source, pair], 0.0)
+                for slot in range(4):
+                    totals[slot] = totals[slot] + jnp.where(block == slot, scale, 0.0) * values
             for slot in range(4):
-                totals[slot] = totals[slot] + jnp.where(block == slot, scale, 0.0) * values
-        for slot in range(4):
-            merged[slot, window] = totals[slot].astype(BF16)
-    send(
-        ("final",), merged.at[pl.ds(2 * (1 - half), 2)], out.at[:, half], {"dp": partner}
-    )
-    last_copy = pltpu.make_async_copy(
-        merged.at[pl.ds(2 * half, 2)], out.at[:, half], local_sem.at[1]
-    )
-    last_copy.start()
+                merged[slot, c, window] = totals[slot].astype(BF16)
+        send(
+            ("final", c),
+            merged.at[pl.ds(2 * (1 - half), 2), c],
+            out.at[:, half, c],
+            {"dp": partner},
+        )
+        last_copies.append(
+            pltpu.make_async_copy(
+                merged.at[pl.ds(2 * half, 2), c], out.at[:, half, c], local_sem.at[2 + c]
+            )
+        )
+        last_copies[c].start()
     for key, copy in copies.items():
         copy.wait_send()
-    last_copy.wait()
-    arrive("final")
+    for c in range(2):
+        last_copies[c].wait()
+        arrive("final", c)
 
 
 def on_device(tokens, w_gate, w_up, w_down, pick_block, pick_live, combine_weight):
@@ -322,16 +347,17 @@
     hid_tiles = group // 128
     hbm = pl.BlockSpec(memory_space=pl.ANY)
     smem = pl.BlockSpec(memory_space=pltpu.SMEM)
-    copy_count = 128
+    copy_count = 144
     result = pl.pallas_call(
         functools.partial(layer_kernel, expert_count),
-        out_shape=jax.ShapeDtypeStruct((2, 2, HALF, lanes), BF16),
+        out_shape=jax.ShapeDtypeStruct((2, 2, 2, HALF // 2, lanes), BF16),
         in_specs=[hbm, hbm, hbm, hbm, smem, smem, smem],
         out_specs=hbm,
         scratch_shapes=[
-            pltpu.VMEM((4, HALF, lanes), BF16),
-            pltpu.VMEM((expert_count, HALF, lanes), BF16),
-            pltpu.VMEM((expert_count, HALF, lanes), BF16),
+            pltpu.VMEM((4, HALF // 2, lanes), BF16),
+            pltpu.VMEM((4, HALF // 2, lanes), BF16),
+            pltpu.VMEM((2, expert_count, HALF // 2, lanes), BF16),
+            pltpu.VMEM((2, expert_count, HALF // 2, lanes), BF16),
             pltpu.VMEM((RING, 2, RING, 2, SUB, width), BF16),
             pltpu.VMEM((hid_tiles, width, 256), BF16),
             pltpu.VMEM((group, width), BF16),
@@ -346,20 +372,20 @@
             pltpu.VMEM((2, 2, SUB, width), BF16),
             pltpu.VMEM((2, SUB, width), BF16),
             pltpu.VMEM((2, SUB, width), BF16),
-            pltpu.VMEM((expert_count, HALF, lanes), BF16),
-            pltpu.VMEM((expert_count, HALF, lanes), BF16),
-            pltpu.VMEM((4, HALF, lanes), BF16),
+            pltpu.VMEM((2, expert_count, HALF // 2, lanes), BF16),
+            pltpu.VMEM((2, expert_count, HALF // 2, lanes), BF16),
+            pltpu.VMEM((4, 2, HALF // 2, lanes), BF16),
             pltpu.SemaphoreType.DMA((copy_count,)),
             pltpu.SemaphoreType.DMA((copy_count,)),
             pltpu.SemaphoreType.DMA((2 * hid_tiles + 1,)),
-            pltpu.SemaphoreType.DMA((2,)),
+            pltpu.SemaphoreType.DMA((4,)),
         ],
         compiler_params=pltpu.CompilerParams(
             collective_id=0, has_side_effects=True, vmem_limit_bytes=60 * 1024 * 1024
         ),
         name="moe_layer",
     )(
-        tokens.reshape(2, 2, HALF, lanes),
+        tokens.reshape(2, 2, 2, HALF // 2, lanes),
         w_gate[0],
         w_up[0],
         w_down[0],

time: 132 us -> 125 us (0.947)
  Pallas kernels: 130 us -> 123 us
    pallas_call x1, Pallas kernels: 130 us -> 123 us  [on_device(): pl.pallas_call(functools.partial(layer_kernel, expert_count), out_shape=j...]
where the time goes in v2:
time: 125 us
  Pallas kernels  123 us (98%)
  local copies, waits for them, and re-layouts  1.67 us (1%)
    pallas_call x1, Pallas kernels, on_device(): pl.pallas_call(functools.partial(layer_kernel, expert_count), out_shape=j...  123 us

profile of v2, /device:TPU:0, one launch (start us, length us, event | category | flops | bytes accessed | tf_op | source)
XLA Modules:
  0.0 124.8 jit_solution(17447362534389766071)
XLA Ops:
  0.0 123.2 %moe_layer.1 = bf16[2,2,2,32,512]{4,3,2,1,0:T(8,128)(2,1)} custom-call(bf16[2,2,2,32,512]{4,3,2,1,0:T(8,128)(2,1)} %bitcast.9, bf16[4096,896]{1,0:T(8,128)(2,1)} %bitcast.5, bf16[4096,896]{1,0:T(8,128)(2,1)} %bitcast.6, bf16[896,4096]{1,0:T(8,128)(2,1)} %bitcast.7, s32[8,8]{1,0:T(8,128)} %pick.1, s32[8,8]{1,0:T(8,128)} %live.1, f32[8,8]{1,0:T(8,128)} %weight.1), custom_call_target="tpu_custom_call" | custom-call | tf_op jit(solution)/shard_map/moe_layer/pallas_call | solution.py:351
  123.2 1.7 %copy.9 = bf16[256,512]{1,0:T(8,128)(2,1)} copy(bf16[256,512]{1,0:T(8,128)(2,1)} %bitcast.8) | data formatting | bytes 524288

commit v3 on v2

--- a/solution.py
+++ b/solution.py
@@ -135,7 +135,7 @@
         chosen = pair_bufs[c][pick[target, pair]].astype(F32)
         return (chosen * live[target, pair].astype(F32)).astype(BF16)
 
-    for c in range(2):
+    def spread_experts(c):
         own_copies[c].wait()
         arrive("pair", c)
         for offset in peers:
@@ -148,6 +148,8 @@
                 {"expert": target},
             )
         arrived[c, expert] = choose(expert, c)
+
+    spread_experts(0)
     for copy in weight_copies:
         copy.start()
 
@@ -175,17 +177,21 @@
         arrive("rows", 1, c, r)
         send(("far", c, r, 1), rows.at[1, c, r, 1], rows.at[3, c, r, 1], {"dp": wide[c][1]})
 
-    def experts(s):
-        group = rows[s].reshape(2 * RING * 2 * SUB, width)
+    def experts(groups, slots):
+        shape = (len(groups), 2, len(slots), 2, SUB)
+        count = len(groups) * len(slots) * 4 * SUB
+        groups = pl.ds(groups[0], len(groups))
+        slots = pl.ds(slots[0], len(slots))
+        batch = rows[groups, :, slots].reshape(count, width)
         for tile in range(hid_tiles):
-            both = jnp.dot(group, w_gu[tile], preferred_element_type=F32)
+            both = jnp.dot(batch, w_gu[tile], preferred_element_type=F32)
             gate = both[:, :128]
             value = gate * (1.0 / (1.0 + jnp.exp(-gate))) * both[:, 128:]
-            hidden[:, tile * 128 : (tile + 1) * 128] = value.astype(BF16)
+            hidden[:count, tile * 128 : (tile + 1) * 128] = value.astype(BF16)
         for tile in range(width // DOWN):
             columns = pl.ds(tile * DOWN, DOWN)
-            value = jnp.dot(hidden[...], w_dn[:, columns], preferred_element_type=F32)
-            part[s, :, :, :, :, columns] = value.astype(BF16).reshape(2, RING, 2, SUB, DOWN)
+            value = jnp.dot(hidden[:count], w_dn[:, columns], preferred_element_type=F32)
+            part[groups, :, slots, :, :, columns] = value.astype(BF16).reshape(*shape, DOWN)
 
     for c in range(2):
         for offset in peers:
@@ -194,6 +200,8 @@
         send(("near", c, 2), rows.at[0, c, 0], rows.at[0, c, 2], {"dp": near[c][0]})
         send(("near", c, 1), rows.at[0, c, 0], rows.at[0, c, 1], {"dp": near[c][1]})
         spread_wide(c, 0)
+        if c == 0:
+            spread_experts(1)
     for c in range(2):
         arrive("near", c, 2)
         send(("nearfar", c, 0), rows.at[0, c, 2, 0], rows.at[0, c, 3, 0], {"dp": near[c][0]})
@@ -210,26 +218,35 @@
         forward_wide(c, 0)
     for copy in weight_copies:
         copy.wait()
-    experts(0)
-    for r in (1, 2, 3):
+    experts((0,), (0, 1, 2, 3))
+    for c in range(2):
+        forward_wide(c, 1)
+    experts((1, 2), (0, 1))
+    for r in (2, 3):
         for c in range(2):
             forward_wide(c, r)
-    experts(1)
+    experts((1, 2), (2, 3))
     for c in range(2):
         send(("half", c, 1), part.at[1, c, :, 1], from_minus.at[c, :, 1], {"dp": wide[c][0]})
-    experts(2)
-    for c in range(2):
         send(("half", c, 0), part.at[2, c, :, 0], from_plus.at[c, :, 0], {"dp": wide[c][1]})
-    for r in range(RING):
-        for c in range(2):
-            arrive("far", c, r, 0)
-            arrive("far", c, r, 1)
-    experts(3)
-    order = (3, 1, 2, 0)
-    for r in order:
-        for c in range(2):
-            send(("sumfar", c, r, 0), part.at[3, c, r, 0], far_minus.at[c, r], {"dp": wide[c][0]})
-            send(("sumfar", c, r, 1), part.at[3, c, r, 1], far_plus.at[c, r], {"dp": wide[c][1]})
+    for slots in ((0, 1), (2, 3)):
+        for r in slots:
+            for c in range(2):
+                arrive("far", c, r, 0)
+                arrive("far", c, r, 1)
+        experts((3,), slots)
+        for r in reversed(slots):
+            for c in range(2):
+                send(
+                    ("sumfar", c, r, 0),
+                    part.at[3, c, r, 0],
+                    far_minus.at[c, r],
+                    {"dp": wide[c][0]},
+                )
+                send(
+                    ("sumfar", c, r, 1), part.at[3, c, r, 1], far_plus.at[c, r], {"dp": wide[c][1]}
+                )
+    order = (1, 3, 2, 0)
     for r in order:
         for c in range(2):
             arrive("sumfar", c, r, 0)

time: 125 us -> 118 us (0.944)
  Pallas kernels: 123 us -> 115 us
    pallas_call x1, Pallas kernels: 123 us -> 115 us  [on_device(): pl.pallas_call(functools.partial(layer_kernel, expert_count), out_shape=j...]
where the time goes in v3:
time: 118 us; the launch traced here: 117 us
  Pallas kernels  115 us (97%)
  local copies, waits for them, and re-layouts  1.67 us (1%)
    pallas_call x1, Pallas kernels, on_device(): pl.pallas_call(functools.partial(layer_kernel, expert_count), out_shape=j...  115 us

profile of v3, /device:TPU:0, one launch (start us, length us, event | category | flops | bytes accessed | tf_op | source)
XLA Modules:
  0.0 116.9 jit_solution(5090329831320526909)
XLA Ops:
  0.0 115.2 %moe_layer.1 = bf16[2,2,2,32,512]{4,3,2,1,0:T(8,128)(2,1)} custom-call(bf16[2,2,2,32,512]{4,3,2,1,0:T(8,128)(2,1)} %bitcast.9, bf16[4096,896]{1,0:T(8,128)(2,1)} %bitcast.5, bf16[4096,896]{1,0:T(8,128)(2,1)} %bitcast.6, bf16[896,4096]{1,0:T(8,128)(2,1)} %bitcast.7, s32[8,8]{1,0:T(8,128)} %pick.1, s32[8,8]{1,0:T(8,128)} %live.1, f32[8,8]{1,0:T(8,128)} %weight.1), custom_call_target="tpu_custom_call" | custom-call | tf_op jit(solution)/shard_map/moe_layer/pallas_call | solution.py:368
  115.2 1.7 %copy.9 = bf16[256,512]{1,0:T(8,128)(2,1)} copy(bf16[256,512]{1,0:T(8,128)(2,1)} %bitcast.8) | data formatting | bytes 524288

commit v4 on v3

--- a/solution.py
+++ b/solution.py
@@ -22,10 +22,13 @@
     w_gate,
     w_up,
     w_down,
+    pick_hbm,
+    live_hbm,
+    weight_hbm,
+    out,
     pick,
     live,
     weight,
-    out,
     pair_first,
     pair_second,
     send_buf,
@@ -83,6 +86,21 @@
     weight_copies.append(pltpu.make_async_copy(w_down, w_dn, weight_sem.at[2 * hid_tiles]))
 
     pair_bufs = (pair_first, pair_second)
+    table_copies = [
+        pltpu.make_async_copy(source, table, local_sem.at[4 + number])
+        for number, (source, table) in enumerate(
+            ((pick_hbm, pick), (live_hbm, live), (weight_hbm, weight))
+        )
+    ]
+    own_copies = [
+        pltpu.make_async_copy(
+            tok.at[:, half, c], pair_bufs[c].at[pl.ds(2 * half, 2)], local_sem.at[c]
+        )
+        for c in range(2)
+    ]
+    for copy in table_copies + own_copies:
+        copy.start()
+
     barrier = pltpu.get_barrier_semaphore()
     for target in (x_plus, x_minus, y_plus, y_minus):
         pl.semaphore_signal(
@@ -122,14 +140,8 @@
             pair_bufs[c].at[pl.ds(2 * half, 2)],
             {"dp": partner},
         )
-    own_copies = [
-        pltpu.make_async_copy(
-            tok.at[:, half, c], pair_bufs[c].at[pl.ds(2 * half, 2)], local_sem.at[c]
-        )
-        for c in range(2)
-    ]
-    for copy in own_copies:
-        copy.start()
+    for copy in table_copies:
+        copy.wait()
 
     def choose(target, c):
         chosen = pair_bufs[c][pick[target, pair]].astype(F32)
@@ -362,15 +374,17 @@
     width = lanes * expert_count
     group = w_gate.shape[2]
     hid_tiles = group // 128
-    hbm = pl.BlockSpec(memory_space=pl.ANY)
-    smem = pl.BlockSpec(memory_space=pltpu.SMEM)
+    hbm = pl.BlockSpec(memory_space=pltpu.HBM)
     copy_count = 144
     result = pl.pallas_call(
         functools.partial(layer_kernel, expert_count),
         out_shape=jax.ShapeDtypeStruct((2, 2, 2, HALF // 2, lanes), BF16),
-        in_specs=[hbm, hbm, hbm, hbm, smem, smem, smem],
-        out_specs=hbm,
+        in_specs=[hbm] * 7,
+        out_specs=pl.BlockSpec(memory_space=pl.ANY),
         scratch_shapes=[
+            pltpu.SMEM(pick_block.shape, pick_block.dtype),
+            pltpu.SMEM(pick_live.shape, pick_live.dtype),
+            pltpu.SMEM(combine_weight.shape, combine_weight.dtype),
             pltpu.VMEM((4, HALF // 2, lanes), BF16),
             pltpu.VMEM((4, HALF // 2, lanes), BF16),
             pltpu.VMEM((2, expert_count, HALF // 2, lanes), BF16),
@@ -395,7 +409,7 @@
             pltpu.SemaphoreType.DMA((copy_count,)),
             pltpu.SemaphoreType.DMA((copy_count,)),
             pltpu.SemaphoreType.DMA((2 * hid_tiles + 1,)),
-            pltpu.SemaphoreType.DMA((4,)),
+            pltpu.SemaphoreType.DMA((7,)),
         ],
         compiler_params=pltpu.CompilerParams(
             collective_id=0, has_side_effects=True, vmem_limit_bytes=60 * 1024 * 1024

time: 118 us -> 117 us (level)
  no operation moved by 1% of the time
where the time goes in v4:
time: 117 us; the launch traced here: 116 us
  Pallas kernels  114 us (97%)
  local copies, waits for them, and re-layouts  1.67 us (1%)
    pallas_call x1, Pallas kernels, on_device(): pl.pallas_call(functools.partial(layer_kernel, expert_count), out_shape=j...  114 us

profile of v4, /device:TPU:0, one launch (start us, length us, event | category | flops | bytes accessed | tf_op | source)
XLA Modules:
  0.0 116.1 jit_solution(4480016613385854334)
XLA Ops:
  0.0 114.4 %moe_layer.1 = bf16[2,2,2,32,512]{4,3,2,1,0:T(8,128)(2,1)} custom-call(bf16[2,2,2,32,512]{4,3,2,1,0:T(8,128)(2,1)} %bitcast.9, bf16[4096,896]{1,0:T(8,128)(2,1)} %bitcast.5, bf16[4096,896]{1,0:T(8,128)(2,1)} %bitcast.6, bf16[896,4096]{1,0:T(8,128)(2,1)} %bitcast.7, s32[8,8]{1,0:T(8,128)} %pick_hbm.1, s32[8,8]{1,0:T(8,128)} %live_hbm.1, f32[8,8]{1,0:T(8,128)} %weight_hbm.1), custom_call_target="tpu_custom_call" | custom-call | tf_op jit(solution)/shard_map/moe_layer/pallas_call | solution.py:379
  114.4 1.7 %copy.9 = bf16[256,512]{1,0:T(8,128)(2,1)} copy(bf16[256,512]{1,0:T(8,128)(2,1)} %bitcast.8) | data formatting | bytes 524288

commit v5 on v4

--- a/solution.py
+++ b/solution.py
@@ -133,13 +133,15 @@
     def arrive(*key):
         copies[key].wait_recv()
 
-    for c in range(2):
+    def swap(c):
         send(
             ("pair", c),
             tok.at[:, 1 - half, c],
             pair_bufs[c].at[pl.ds(2 * half, 2)],
             {"dp": partner},
         )
+
+    swap(0)
     for copy in table_copies:
         copy.wait()
 
@@ -150,6 +152,8 @@
     def spread_experts(c):
         own_copies[c].wait()
         arrive("pair", c)
+        if c == 0:
+            swap(1)
         for offset in peers:
             target = lax.rem(expert + offset, expert_count)
             send_buf[c, offset] = choose(target, c)
@@ -219,13 +223,14 @@
         send(("nearfar", c, 0), rows.at[0, c, 2, 0], rows.at[0, c, 3, 0], {"dp": near[c][0]})
         arrive("near", c, 1)
         send(("nearfar", c, 1), rows.at[0, c, 1, 1], rows.at[0, c, 3, 1], {"dp": near[c][1]})
-    for r in (1, 2):
-        for c in range(2):
-            spread_wide(c, r)
+    for c in range(2):
+        spread_wide(c, 1)
     for c in range(2):
         arrive("nearfar", c, 0)
         arrive("nearfar", c, 1)
         spread_wide(c, 3)
+    for c in range(2):
+        spread_wide(c, 2)
     for c in range(2):
         forward_wide(c, 0)
     for copy in weight_copies:

time: 117 us -> 117 us (level)
  no operation moved by 1% of the time
where the time goes in v5:
time: 117 us; the launch traced here: 116 us
  Pallas kernels  114 us (97%)
  local copies, waits for them, and re-layouts  1.67 us (1%)
    pallas_call x1, Pallas kernels, on_device(): pl.pallas_call(functools.partial(layer_kernel, expert_count), out_shape=j...  114 us

profile of v5, /device:TPU:0, one launch (start us, length us, event | category | flops | bytes accessed | tf_op | source)
XLA Modules:
  0.0 115.7 jit_solution(8474648980522889300)
XLA Ops:
  0.0 114.0 %moe_layer.1 = bf16[2,2,2,32,512]{4,3,2,1,0:T(8,128)(2,1)} custom-call(bf16[2,2,2,32,512]{4,3,2,1,0:T(8,128)(2,1)} %bitcast.9, bf16[4096,896]{1,0:T(8,128)(2,1)} %bitcast.5, bf16[4096,896]{1,0:T(8,128)(2,1)} %bitcast.6, bf16[896,4096]{1,0:T(8,128)(2,1)} %bitcast.7, s32[8,8]{1,0:T(8,128)} %pick_hbm.1, s32[8,8]{1,0:T(8,128)} %live_hbm.1, f32[8,8]{1,0:T(8,128)} %weight_hbm.1), custom_call_target="tpu_custom_call" | custom-call | tf_op jit(solution)/shard_map/moe_layer/pallas_call | solution.py:384
  114.0 1.7 %copy.9 = bf16[256,512]{1,0:T(8,128)(2,1)} copy(bf16[256,512]{1,0:T(8,128)(2,1)} %bitcast.8) | data formatting | bytes 524288
